TPU v7x, 32 devices: a whole 2x2x4 slice. The times are simulated.
32 devices in a mesh: row: 4 (over y, x), col: 8 (over z, core).
Axes of the slice: x: 2, y: 2, z: 4, core: 2. Of those that a mesh axis runs over, the one named last changes fastest.
Arguments:
- matrix: float32 [256, 40960], P('row', 'col'), as said below
- pivots: int32 [256], replicated, may hold values from 0 to 255, as said below
- check_weights: float32 [2, 256], P(None, 'row'), may hold values from -0.375 to 0.375
- checksum: float32 [2, 40960], P(None, 'col'), may hold values from -6 to 6
- coefficients: float32 [4, 8], P('row', 'col'), may hold values from 0.125 to 0.5
- checkpoints: int32 [4, 2], P('row'), may hold values from 0 to 3, as said below
Outputs:
- updated: float32 [256, 40960], P('row', 'col')
- new_checksum: float32 [2, 40960], P(None, 'col')
- parity: float32 [256, 40960], P('row', 'col')
Inputs may be any that keep to these rules, and one draw needn't show every extreme that they name: `pivots`: 256 distinct row numbers. `checkpoints`: row index 0 keeps both codes on member 4 - 1, row index 1 on member 0. `matrix`: the first 256 columns are the panel's multipliers, of size about 256 ** -0.5.
All inputs are finite; a program needn't handle non-finite values.
Results may differ from a plain program's by a relative error of at most 0.000098.
Values sent between devices are 32-bit elements; how exact they have to be, the bound alone decides.
No kernel may reach another device: no remote copies, remote signals or barrier semaphores. Data moves between devices by JAX's collectives and lax.ppermute only.
A program may use at most 64 MiB of HBM per device.

v0:
```python
import jax
import jax.numpy as jnp
from jax import lax
from jax.sharding import PartitionSpec as P


def spread(value, axis, source):
    kept = jnp.where(lax.axis_index(axis) == source, value, 0).astype(value.dtype)
    return lax.psum(kept, axis)


def from_partner(block, axis, bit):
    count = lax.axis_size(axis)
    route = []
    for low in range(count):
        high = low | 1 << bit
        if high != low and high < count:
            route += [(low, high), (high, low)]
    return lax.ppermute(block, axis, route)


def per_device(matrix, pivots, check_weights, checksum, coefficients, checkpoints):
    rows_local = matrix.shape[0]
    cols_local = matrix.shape[1]
    width = pivots.shape[0]
    checks = check_weights.shape[0]
    row_index = lax.axis_index("row")
    col_index = lax.axis_index("col")
    lower = spread(matrix[:, :width], "col", 0)
    local_rows = pivots - row_index * rows_local
    selector = (local_rows[:, None] == jnp.arange(rows_local, dtype=jnp.int32)[None, :]).astype(
        jnp.float32
    )
    picked = jnp.dot(
        selector, matrix, preferred_element_type=jnp.float32, precision=lax.Precision.HIGHEST
    )
    weighted_part = jnp.dot(
        check_weights, lower, preferred_element_type=jnp.float32, precision=lax.Precision.HIGHEST
    )
    padded_part = jnp.pad(weighted_part, ((0, 0), (0, cols_local - width)))
    stacked = lax.psum(jnp.concatenate([picked, padded_part], axis=0), "row")
    picked = stacked[:width]
    weighted_lower = stacked[width : width + checks, :width]
    column_ids = col_index * cols_local + jnp.arange(cols_local, dtype=jnp.int32)
    upper = jnp.where(column_ids[None, :] >= width, picked, jnp.float32(0.0))
    updated = matrix - jnp.dot(
        lower, upper, preferred_element_type=jnp.float32, precision=lax.Precision.HIGHEST
    )
    new_checksum = checksum - jnp.dot(
        weighted_lower, upper, preferred_element_type=jnp.float32, precision=lax.Precision.HIGHEST
    )
    own = matrix * coefficients[0, 0]
    position = col_index // 2
    group_id = col_index % 2
    keeper = jnp.where(group_id == 0, checkpoints[0, 0], checkpoints[0, 1])
    levels = lax.axis_size("col").bit_length() - 1
    piece = own
    for level in range(1, levels):
        half = piece.shape[1] // 2
        bit_value = col_index // 2**level % 2
        first_half = piece[:, :half]
        second_half = piece[:, half:]
        outgoing = jnp.where(bit_value == 0, second_half, first_half)
        kept = jnp.where(bit_value == 0, first_half, second_half)
        piece = kept + from_partner(outgoing, "col", level)
    for level in range(levels - 1, 0, -1):
        bit_value = col_index // 2**level % 2
        partner = from_partner(piece, "col", level)
        piece = jnp.where(
            bit_value == 0,
            jnp.concatenate([piece, partner], axis=1),
            jnp.concatenate([partner, piece], axis=1),
        )
    parity = jnp.where(position == keeper, piece, jnp.float32(0.0))
    return (updated, new_checksum, parity)


def solution(mesh):
    in_specs = (
        P("row", "col"),
        P(),
        P(None, "row"),
        P(None, "col"),
        P("row", "col"),
        P("row", None),
    )
    out_specs = (P("row", "col"), P(None, "col"), P("row", "col"))
    return jax.shard_map(
        per_device, mesh=mesh, in_specs=in_specs, out_specs=out_specs, check_vma=False
    )
```

profile of v0, /device:TPU:0, one launch (start us, length us, event | category | flops | bytes accessed | tf_op | source)
XLA Modules:
  0.0 215.2 jit_solution(14134000331034751280)
XLA Ops:
  7.2 0.0 all-reduce.4.cloned.1.call-start
  7.2 1.5 slice_select_fusion.5
  8.7 0.0 all-reduce.6.cloned.1.call-start
  9.5 1.5 broadcast_multiply_fusion
  11.0 0.2 copy-done.2
  11.2 4.6 %fusion.5 = f32[256,5120]{1,0:T(8,128)} fusion(f32[64,5120]{1,0:T(8,128)S(1)} %copy-done.2, s32[256]{0:T(256)S(1)} %broadcast_subtract_fusion), kind=kOutput, calls=%fused_computation.19 | convolution fusion | flops 1006649344 | bytes 6554624 | tf_op jit(solution)/shard_map/dot_general | solution.py:34
  15.7 52.6 %all-reduce.4.cloned.1.call-done = f32[64,256]{1,0:T(8,128)} async-done(((f32[64,256]{1,0:T(8,128)}), f32[64,256]{1,0:T(8,128)}) %all-reduce.4.cloned.1.call-update) | async-done | bytes 65552 | tf_op jit(solution)/shard_map/psum | solution.py:9
  68.3 1.0 convolution_bitcast_fusion
  69.3 5.6 %select_maximum_fusion = f32[258,5120]{1,0:T(8,128)} fusion(f32[2,256]{1,0:T(2,128)S(1)} %convolution_bitcast_fusion, f32[256,5120]{1,0:T(8,128)} %fusion.5), kind=kLoop, calls=%fused_computation.2 | loop fusion | flops 3962880 | bytes 10528768 | tf_op jit(solution)/shard_map/concatenate | solution.py:41
  74.9 0.1 slice_select_fusion.3
  75.0 0.6 collective-permute-start
  75.6 14.3 %collective-permute-done = f32[64,2560]{1,0:T(8,128)} collective-permute-done((f32[64,2560]{1,0:T(8,128)S(1)}, f32[64,2560]{1,0:T(8,128)}, u32[]{:S(2)}, u32[]{:S(2)}) %collective-permute-start) | collective-permute-done | bytes 655392 | tf_op jit(solution)/shard_map/ppermute | solution.py:19
  89.9 1.4 select_add_fusion
  91.3 1.2 collective-permute-start.1
  92.5 13.6 %collective-permute-done.1 = f32[64,1280]{1,0:T(8,128)S(1)} collective-permute-done((f32[64,1280]{1,0:T(8,128)S(1)}, f32[64,1280]{1,0:T(8,128)S(1)}, u32[]{:S(2)}, u32[]{:S(2)}) %collective-permute-start.1) | collective-permute-done | bytes 327712 | tf_op jit(solution)/shard_map/ppermute | solution.py:19
  106.2 0.1 collective-permute-start.2
  106.2 16.8 %collective-permute-done.2 = f32[64,1280]{1,0:T(8,128)S(1)} collective-permute-done((f32[64,1280]{1,0:T(8,128)S(1)}, f32[64,1280]{1,0:T(8,128)S(1)}, u32[]{:S(2)}, u32[]{:S(2)}) %collective-permute-start.2) | collective-permute-done | bytes 327712 | tf_op jit(solution)/shard_map/ppermute | solution.py:19
  123.1 0.1 collective-permute-start.3
  123.2 0.6 fusion.10
  125.1 14.3 %collective-permute-done.3 = f32[64,2560]{1,0:T(8,128)S(1)} collective-permute-done((f32[64,2560]{1,0:T(8,128)S(1)}, f32[64,2560]{1,0:T(8,128)S(1)}, u32[]{:S(2)}, u32[]{:S(2)}) %collective-permute-start.3) | collective-permute-done | bytes 655392 | tf_op jit(solution)/shard_map/ppermute | solution.py:19
  139.4 1.2 fusion.4
  140.6 57.4 %all-reduce.6.cloned.1.call-done = f32[258,5120]{1,0:T(8,128)} async-done(((f32[258,5120]{1,0:T(8,128)}), f32[258,5120]{1,0:T(8,128)}) %all-reduce.6.cloned.1.call-update) | async-done | bytes 5283856 | tf_op jit(solution)/shard_map/psum | solution.py:41
  197.9 7.1 %convolution_subtract_fusion = f32[64,5120]{1,0:T(8,128)} fusion(f32[64,5120]{1,0:T(8,128)S(1)} %copy-done.2, f32[64,256]{1,0:T(8,128)S(1)} %copy-done.3, f32[258,5120]{1,0:T(8,128)} %all-reduce.6.cloned.1.call-done, pred[5120]{0:T(1024)(128)(4,1)S(1)} %add_compare_fusion), kind=kOutput, calls=%fused_computation | convolution fusion | flops 1008271360 | bytes 7934976 | tf_op jit(solution)/shard_map/dot_general | solution.py:46
  205.0 3.3 %convolution_subtract_fusion.1 = f32[2,5120]{1,0:T(2,128)} fusion(f32[2,5120]{1,0:T(2,128)S(1)} %copy-done.4, f32[258,5120]{1,0:T(8,128)S(1)} %copy-done.1, pred[5120]{0:T(1024)(128)(4,1)S(1)} %add_compare_fusion), kind=kOutput, calls=%fused_computation.1 | convolution fusion | flops 32778240 | bytes 5331968 | tf_op jit(solution)/shard_map/dot_general | solution.py:49
  (20 shorter events, 0.2 us)
Async XLA Ops:
  7.2 61.2 %copy-start = (f32[2,64]{1,0:T(2,128)S(1)}, f32[2,64]{1,0:T(2,128)}, u32[]{:S(2)}) copy-start(f32[2,64]{1,0:T(2,128)} %param.8) | copy-start | bytes 1540
  7.2 61.1 %all-reduce.4.cloned.1.call-start = ((), (), s32[]{:S(2)}) async-start(), calls=%async_computation | async-start | bytes 131072 | tf_op jit(solution)/shard_map/psum | solution.py:9
  8.7 189.2 %all-reduce.6.cloned.1.call-start = ((), (), s32[]{:S(2)}) async-start(), calls=%async_computation.1 | async-start | bytes 10813440 | tf_op jit(solution)/shard_map/psum | solution.py:41
  9.4 1.6 copy-start.6
  9.4 1.7 copy-start.2
  75.0 14.9 %collective-permute-start = (f32[64,2560]{1,0:T(8,128)S(1)}, f32[64,2560]{1,0:T(8,128)}, u32[]{:S(2)}, u32[]{:S(2)}) collective-permute-start(f32[64,2560]{1,0:T(8,128)S(1)} %slice_select_fusion.3), channel_id=1, source_target_pairs={{0,2},{2,0},{1,3},{3,1},{4,6},{6,4},{5,7},{7,5},{8,10},{10,8},{9,1... | collective-permute-start | bytes 1966088 | tf_op jit(solution)/shard_map/ppermute | solution.py:19
  91.3 31.9 %copy-start.5 = (s32[1,2]{1,0:T(1,128)S(1)}, s32[1,2]{1,0:T(1,128)}, u32[]{:S(2)}) copy-start(s32[1,2]{1,0:T(1,128)} %param.11) | copy-start | bytes 28
  91.3 14.8 %collective-permute-start.1 = (f32[64,1280]{1,0:T(8,128)S(1)}, f32[64,1280]{1,0:T(8,128)S(1)}, u32[]{:S(2)}, u32[]{:S(2)}) collective-permute-start(f32[64,1280]{1,0:T(8,128)S(1)} %slice_select_fusion.4), channel_id=1, source_target_pairs={{0,4},{4,0},{1,5},{5,1},{2,6},{6,2},{3,7},{7,3},{8,12},{12,8},{9,1... | collective-permute-start | bytes 983048 | tf_op jit(solution)/shard_map/ppermute | solution.py:19
  106.2 16.9 %collective-permute-start.2 = (f32[64,1280]{1,0:T(8,128)S(1)}, f32[64,1280]{1,0:T(8,128)S(1)}, u32[]{:S(2)}, u32[]{:S(2)}) collective-permute-start(f32[64,1280]{1,0:T(8,128)S(1)} %select_add_fusion.1), channel_id=1, source_target_pairs={{0,4},{4,0},{1,5},{5,1},{2,6},{6,2},{3,7},{7,3},{8,12},{12,8},{9,1... | collective-permute-start | bytes 983048 | tf_op jit(solution)/shard_map/ppermute | solution.py:19
  123.1 16.3 %collective-permute-start.3 = (f32[64,2560]{1,0:T(8,128)S(1)}, f32[64,2560]{1,0:T(8,128)S(1)}, u32[]{:S(2)}, u32[]{:S(2)}) collective-permute-start(f32[64,2560]{1,0:T(8,128)S(1)} %maximum_select_fusion.1), channel_id=1, source_target_pairs={{0,2},{2,0},{1,3},{3,1},{4,6},{6,4},{5,7},{7,5},{8,10},{10,8},{9,1... | collective-permute-start | bytes 1966088 | tf_op jit(solution)/shard_map/ppermute | solution.py:19
  125.1 72.8 %copy-start.3 = (f32[64,256]{1,0:T(8,128)S(1)}, f32[64,256]{1,0:T(8,128)}, u32[]{:S(2)}) copy-start(f32[64,256]{1,0:T(8,128)} %all-reduce.4.cloned.1.call-done) | copy-start | bytes 196612
  140.6 64.4 %copy-start.4 = (f32[2,5120]{1,0:T(2,128)S(1)}, f32[2,5120]{1,0:T(2,128)}, u32[]{:S(2)}) copy-start(f32[2,5120]{1,0:T(2,128)} %param.9) | copy-start | bytes 122884
  197.9 7.1 %copy-start.1 = (f32[258,5120]{1,0:T(8,128)S(1)}, f32[258,5120]{1,0:T(8,128)}, u32[]{:S(2)}) copy-start(f32[258,5120]{1,0:T(8,128)} %all-reduce.6.cloned.1.call-done) | copy-start | bytes 15851524
Sparse Core Ops, SparseCore 0:
  10.9 57.4 all-reduce.3
  75.0 122.8 all-reduce.5
where the time goes:
time: 216 us; the launch traced here: 215 us
  waiting for transfers between devices  169 us (78%)
  between operations  16.1 us (7%)
  matrix products  15.9 us (7%)
  other arithmetic  11.3 us (5%)
    ppermute x4, waiting for transfers between devices, from_partner(): return lax.ppermute(block, axis, route)  59 us
    psum x1, waiting for transfers between devices, per_device(): stacked = lax.psum(jnp.concatenate([picked, padded_part], axis=0), 'row')  57.4 us
    psum x1, waiting for transfers between devices, spread(): return lax.psum(kept, axis)  52.6 us
    dot_general x1, matrix products, per_device(): jnp.dot(lower, upper, preferred_element_type=jnp.float32, precision=lax.P...  7.08 us
    concatenate x1, other arithmetic, per_device(): stacked = lax.psum(jnp.concatenate([picked, padded_part], axis=0), 'row')  5.58 us
    dot_general x1, matrix products, per_device(): jnp.dot(selector, matrix, preferred_element_type=jnp.float32, precision=l...  4.57 us
  transfers between devices with their start and end apart: 6, of which 6 were waited for; matrix products, arithmetic and copies ran while one was open for 4% of the time, Pallas kernels for 0%

commit v1 on v0

--- a/solution.py
+++ b/solution.py
@@ -38,7 +38,9 @@
         check_weights, lower, preferred_element_type=jnp.float32, precision=lax.Precision.HIGHEST
     )
     padded_part = jnp.pad(weighted_part, ((0, 0), (0, cols_local - width)))
-    stacked = lax.psum(jnp.concatenate([picked, padded_part], axis=0), "row")
+    own_2 = jnp.concatenate([picked, padded_part], axis=0)
+    pieces = lax.all_gather(own_2, "row")
+    stacked = jnp.sum(pieces, axis=0)
     picked = stacked[:width]
     weighted_lower = stacked[width : width + checks, :width]
     column_ids = col_index * cols_local + jnp.arange(cols_local, dtype=jnp.int32)

time: 216 us -> 304 us (1.41)
  waiting for transfers between devices: 169 us -> 242 us
  other arithmetic: 11.3 us -> 22.1 us
  matrix products: 15.9 us -> 19.6 us
    all_gather x0 -> x1, waiting for transfers between devices: none -> 130 us  [per_device(): pieces = lax.all_gather(own_2, 'row')]
    psum x1 -> x0, waiting for transfers between devices: 57.4 us -> none  [per_device(): stacked = lax.psum(jnp.concatenate([picked, padded_part], axis=0), 'row')]
    reduce_sum x0 -> x1, other arithmetic: none -> 11.4 us  [per_device(): stacked = jnp.sum(pieces, axis=0)]
    concatenate x1 -> x0, other arithmetic: 5.58 us -> none  [per_device(): stacked = lax.psum(jnp.concatenate([picked, padded_part], axis=0), 'row')]
    unnamed x0 -> x1, other arithmetic: none -> 5.55 us
  transfers between devices with their start and end apart: 6 -> 6, of which waited for: 6 -> 6; matrix products, arithmetic and copies ran while one was open for 4% -> 3% of each run, Pallas kernels for 0% -> 0%
where the time goes in v1:
time: 304 us
  waiting for transfers between devices  242 us (80%)
  other arithmetic  22.1 us (7%)
  matrix products  19.6 us (6%)
  between operations  16.2 us (5%)
    all_gather x1, waiting for transfers between devices, per_device(): pieces = lax.all_gather(own_2, 'row')  130 us
    ppermute x4, waiting for transfers between devices, from_partner(): return lax.ppermute(block, axis, route)  59 us
    psum x1, waiting for transfers between devices, spread(): return lax.psum(kept, axis)  53 us
    reduce_sum x1, other arithmetic, per_device(): stacked = jnp.sum(pieces, axis=0)  11.4 us
    dot_general x1, matrix products, per_device(): jnp.dot(lower, upper, preferred_element_type=jnp.float32, precision=lax.P...  6.93 us
  transfers between devices with their start and end apart: 6, of which 6 were waited for; matrix products, arithmetic and copies ran while one was open for 3% of the time, Pallas kernels for 0%

profile of v1, /device:TPU:0, one launch (start us, length us, event | category | flops | bytes accessed | tf_op | source)
XLA Modules:
  0.0 303.6 jit_solution(14740598045898511997)
XLA Ops:
  7.2 1.5 slice_select_fusion.5
  8.8 0.7 broadcast_subtract_fusion
  9.5 5.9 %fusion.6 = f32[256,5120]{1,0:T(8,128)} fusion(f32[64,5120]{1,0:T(8,128)} %param.6, s32[256]{0:T(256)S(1)} %broadcast_subtract_fusion), kind=kOutput, calls=%fused_computation.20 | convolution fusion | flops 1006649344 | bytes 6554624 | tf_op jit(solution)/shard_map/dot_general | solution.py:34
  15.3 53.0 %all-reduce.3.cloned.1.call-done = f32[64,256]{1,0:T(8,128)} async-done(((f32[64,256]{1,0:T(8,128)}), f32[64,256]{1,0:T(8,128)}) %all-reduce.3.cloned.1.call-update) | async-done | bytes 65552 | tf_op jit(solution)/shard_map/psum | solution.py:9
  68.3 1.0 convolution_bitcast_fusion
  69.3 5.6 %fusion = f32[1,258,5120]{2,1,0:T(8,128)} fusion(f32[2,256]{1,0:T(2,128)S(1)} %convolution_bitcast_fusion, f32[256,5120]{1,0:T(8,128)} %fusion.6), kind=kLoop, calls=%fused_computation.3 | loop fusion | flops 3962880 | bytes 10528768
  75.7 0.5 copy-done.1
  76.2 0.1 broadcast_multiply_fusion
  76.3 0.1 slice_select_fusion.3
  76.4 0.6 collective-permute-start
  77.0 14.3 %collective-permute-done = f32[64,2560]{1,0:T(8,128)} collective-permute-done((f32[64,2560]{1,0:T(8,128)S(1)}, f32[64,2560]{1,0:T(8,128)}, u32[]{:S(2)}, u32[]{:S(2)}) %collective-permute-start) | collective-permute-done | bytes 655392 | tf_op jit(solution)/shard_map/ppermute | solution.py:19
  91.3 1.4 select_add_fusion
  92.8 1.3 collective-permute-start.1
  94.1 13.4 %collective-permute-done.1 = f32[64,1280]{1,0:T(8,128)S(1)} collective-permute-done((f32[64,1280]{1,0:T(8,128)S(1)}, f32[64,1280]{1,0:T(8,128)S(1)}, u32[]{:S(2)}, u32[]{:S(2)}) %collective-permute-start.1) | collective-permute-done | bytes 327712 | tf_op jit(solution)/shard_map/ppermute | solution.py:19
  107.6 0.1 collective-permute-start.2
  107.7 16.8 %collective-permute-done.2 = f32[64,1280]{1,0:T(8,128)S(1)} collective-permute-done((f32[64,1280]{1,0:T(8,128)S(1)}, f32[64,1280]{1,0:T(8,128)S(1)}, u32[]{:S(2)}, u32[]{:S(2)}) %collective-permute-start.2) | collective-permute-done | bytes 327712 | tf_op jit(solution)/shard_map/ppermute | solution.py:19
  124.6 0.1 collective-permute-start.3
  124.7 0.6 fusion.11
  126.6 14.5 %collective-permute-done.3 = f32[64,2560]{1,0:T(8,128)S(1)} collective-permute-done((f32[64,2560]{1,0:T(8,128)S(1)}, f32[64,2560]{1,0:T(8,128)S(1)}, u32[]{:S(2)}, u32[]{:S(2)}) %collective-permute-start.3) | collective-permute-done | bytes 655392 | tf_op jit(solution)/shard_map/ppermute | solution.py:19
  141.0 1.2 fusion.5
  142.2 130.3 %all-gather.4.cloned.1.call-done = f32[4,258,5120]{2,1,0:T(8,128)} async-done(((f32[1,258,5120]{2,1,0:T(8,128)}), f32[4,258,5120]{2,1,0:T(8,128)}) %all-gather.4.cloned.1.call-update) | async-done | bytes 21135376 | tf_op jit(solution)/shard_map/all_gather | solution.py:42
  272.6 11.4 %reduce_sum.9 = f32[258,5120]{1,0:T(8,128)} reduce(f32[4,258,5120]{2,1,0:T(8,128)} %all-gather.4.cloned.1.call-done, f32[]{:T(128)} %constant.61.clone.1), dimensions={0}, to_apply=%region_1.2 | reduce | flops 3962880 | bytes 26419204 | tf_op jit(solution)/shard_map/reduce_sum | solution.py:43
  284.0 5.8 %convolution_subtract_fusion.1 = f32[2,5120]{1,0:T(2,128)} fusion(f32[2,5120]{1,0:T(2,128)S(1)} %copy-done.3, f32[258,5120]{1,0:T(8,128)} %reduce_sum.9, pred[5120]{0:T(1024)(128)(4,1)S(1)} %add_compare_fusion), kind=kOutput, calls=%fused_computation.1 | convolution fusion | flops 32778240 | bytes 5331968 | tf_op jit(solution)/shard_map/dot_general | solution.py:51
  289.8 6.9 %convolution_subtract_fusion = f32[64,5120]{1,0:T(8,128)} fusion(f32[64,5120]{1,0:T(8,128)S(1)} %copy-done.1, f32[64,256]{1,0:T(8,128)S(1)} %copy-done.2, f32[258,5120]{1,0:T(8,128)} %reduce_sum.9, pred[5120]{0:T(1024)(128)(4,1)S(1)} %add_compare_fusion), kind=kOutput, calls=%fused_computation | convolution fusion | flops 1008271360 | bytes 7934976 | tf_op jit(solution)/shard_map/dot_general | solution.py:48
  (17 shorter events, 0.3 us)
Async XLA Ops:
  7.2 61.2 %copy-start = (f32[2,64]{1,0:T(2,128)S(1)}, f32[2,64]{1,0:T(2,128)}, u32[]{:S(2)}) copy-start(f32[2,64]{1,0:T(2,128)} %param.8) | copy-start | bytes 1540
  7.2 61.1 %all-reduce.3.cloned.1.call-start = ((), (), s32[]{:S(2)}) async-start(), calls=%async_computation | async-start | bytes 131072 | tf_op jit(solution)/shard_map/psum | solution.py:9
  8.7 263.8 %all-gather.4.cloned.1.call-start = ((), (), s32[]{:S(2)}) async-start(), calls=%async_computation.1 | async-start | bytes 27033600 | tf_op jit(solution)/shard_map/all_gather | solution.py:42
  74.9 1.3 copy-start.1
  76.4 14.9 %collective-permute-start = (f32[64,2560]{1,0:T(8,128)S(1)}, f32[64,2560]{1,0:T(8,128)}, u32[]{:S(2)}, u32[]{:S(2)}) collective-permute-start(f32[64,2560]{1,0:T(8,128)S(1)} %slice_select_fusion.3), channel_id=1, source_target_pairs={{0,2},{2,0},{1,3},{3,1},{4,6},{6,4},{5,7},{7,5},{8,10},{10,8},{9,1... | collective-permute-start | bytes 1966088 | tf_op jit(solution)/shard_map/ppermute | solution.py:19
  92.8 31.9 %copy-start.4 = (s32[1,2]{1,0:T(1,128)S(1)}, s32[1,2]{1,0:T(1,128)}, u32[]{:S(2)}) copy-start(s32[1,2]{1,0:T(1,128)} %param.11) | copy-start | bytes 28
  92.8 14.8 %collective-permute-start.1 = (f32[64,1280]{1,0:T(8,128)S(1)}, f32[64,1280]{1,0:T(8,128)S(1)}, u32[]{:S(2)}, u32[]{:S(2)}) collective-permute-start(f32[64,1280]{1,0:T(8,128)S(1)} %slice_select_fusion.4), channel_id=1, source_target_pairs={{0,4},{4,0},{1,5},{5,1},{2,6},{6,2},{3,7},{7,3},{8,12},{12,8},{9,1... | collective-permute-start | bytes 983048 | tf_op jit(solution)/shard_map/ppermute | solution.py:19
  107.6 16.9 %collective-permute-start.2 = (f32[64,1280]{1,0:T(8,128)S(1)}, f32[64,1280]{1,0:T(8,128)S(1)}, u32[]{:S(2)}, u32[]{:S(2)}) collective-permute-start(f32[64,1280]{1,0:T(8,128)S(1)} %select_add_fusion.1), channel_id=1, source_target_pairs={{0,4},{4,0},{1,5},{5,1},{2,6},{6,2},{3,7},{7,3},{8,12},{12,8},{9,1... | collective-permute-start | bytes 983048 | tf_op jit(solution)/shard_map/ppermute | solution.py:19
  124.6 16.5 %collective-permute-start.3 = (f32[64,2560]{1,0:T(8,128)S(1)}, f32[64,2560]{1,0:T(8,128)S(1)}, u32[]{:S(2)}, u32[]{:S(2)}) collective-permute-start(f32[64,2560]{1,0:T(8,128)S(1)} %maximum_select_fusion.1), channel_id=1, source_target_pairs={{0,2},{2,0},{1,3},{3,1},{4,6},{6,4},{5,7},{7,5},{8,10},{10,8},{9,1... | collective-permute-start | bytes 1966088 | tf_op jit(solution)/shard_map/ppermute | solution.py:19
  142.2 141.8 %copy-start.3 = (f32[2,5120]{1,0:T(2,128)S(1)}, f32[2,5120]{1,0:T(2,128)}, u32[]{:S(2)}) copy-start(f32[2,5120]{1,0:T(2,128)} %param.9) | copy-start | bytes 122884
  284.0 5.8 %copy-start.2 = (f32[64,256]{1,0:T(8,128)S(1)}, f32[64,256]{1,0:T(8,128)}, u32[]{:S(2)}) copy-start(f32[64,256]{1,0:T(8,128)} %all-reduce.3.cloned.1.call-done) | copy-start | bytes 196612
Sparse Core Ops, SparseCore 0:
  10.9 57.4 all-reduce.2
  75.0 197.4 all-gather.3
